TPU v7x, 32 devices: a whole 2x2x4 slice. The times are simulated.
32 devices in a mesh: groups: 2 (over y), seq: 8 (over z, core), heads: 2 (over x), sub: 1.
Axes of the slice: x: 2, y: 2, z: 4, core: 2. Of those that a mesh axis runs over, the one named last changes fastest.
Arguments:
- video_q: bfloat16 [5120, 2048], P(('groups', 'seq'), ('heads', 'sub')), parts along dimension 0, may hold values from -10 to 10
- video_cross_keys: bfloat16 [5120, 2048], P(('groups', 'seq'), ('heads', 'sub')), parts along dimension 0, may hold values from -10 to 10
- video_v: bfloat16 [5120, 2048], P(('groups', 'seq'), ('heads', 'sub')), parts along dimension 0, may hold values from -6 to 6
- audio_q: bfloat16 [1280, 2048], P(('groups', 'seq'), ('heads', 'sub')), parts along dimension 0, may hold values from -10 to 10
- audio_k: bfloat16 [1280, 2048], P(('groups', 'seq'), ('heads', 'sub')), parts along dimension 0, may hold values from -10 to 10
- audio_v: bfloat16 [1280, 2048], P(('groups', 'seq'), ('heads', 'sub')), parts along dimension 0, may hold values from -6 to 6
- audio_self_q: bfloat16 [1280, 2048], P(('groups', 'seq'), ('heads', 'sub')), parts along dimension 0, may hold values from -10 to 10
- audio_self_keys: bfloat16 [1280, 2048], P(('groups', 'seq'), ('heads', 'sub')), parts along dimension 0, may hold values from -10 to 10
- audio_self_v: bfloat16 [1280, 2048], P(('groups', 'seq'), ('heads', 'sub')), parts along dimension 0, may hold values from -6 to 6
- video_counts: int32 [16], P('groups'), parts along dimension 0, may hold values from 1 to 320, 2048 in all
- audio_counts: int32 [16], P('groups'), parts along dimension 0, may hold values from 1 to 80, 512 in all
- window_start: int32 [16], P('groups'), parts along dimension 0, may hold values from 0 to 3, as said below
- window_end: int32 [16], P('groups'), parts along dimension 0, may hold values from 1 to 4, as said below
Outputs:
- video_out: bfloat16 [5120, 2048], P(('groups', 'seq'), ('heads', 'sub')), parts along dimension 0
- audio_out: bfloat16 [1280, 2048], P(('groups', 'seq'), ('heads', 'sub')), parts along dimension 0
There are 2 independent parts, one for each index of `groups`. A program takes and returns all parts, laid end to end along the dimension named above; each array names one. Nothing has to cross between parts.
Inputs may be any that keep to these rules, and one draw needn't show every extreme that they name: `video_counts`: the live tokens of each seq index's block of slots come first in it. `audio_counts`: the live tokens of each seq index's block of slots come first in it. window_start[f] is f // 2 or one less, never below 0, except for the frames with f // 2 = 2, whose window holds all 4 blocks. window_end[f] is f // 2 plus one or two, never above 4, except for the frames whose window holds all blocks.
All inputs are finite; a program needn't handle non-finite values.
Results may differ from a plain program's by a relative error of at most 0.0085.
Values may be sent and summed in bfloat16 or wider, within the bound.
A program may use at most 64 MiB of HBM per device.

v0:
```python
import jax
import jax.numpy as jnp
from jax import lax
from jax.sharding import PartitionSpec as P

HD = 64
FRAME_TOKENS = 256
AUDIO_WIN_BLOCK = 128


NEG = -1e30


def lookup(table, index):
    hits = index[:, None] == jnp.arange(table.shape[0], dtype=jnp.int32)[None, :]
    return jnp.sum(jnp.where(hits, table[None, :], 0), axis=1)


def slot_info(counts, index, capacity):
    owner = index // capacity
    place = index - owner * capacity
    starts = jnp.cumsum(counts) - counts
    live = place < lookup(counts, owner)
    position = lookup(starts, owner) + place
    return (live, position)


def split_size(total, limit):
    amount = total
    while amount > limit and amount % 2 == 0:
        amount = amount // 2
    return amount


def attend_block(state, query, key_rows, values, allowed):
    highest, total, mixed = state
    scores = jnp.einsum(
        "qhd,khd->qhk", query, key_rows, preferred_element_type=jnp.float32
    ) * query.shape[2] ** (-0.5)
    scores = jnp.where(allowed[:, None, :], scores, NEG)
    newest = jnp.maximum(highest, jnp.max(scores, axis=2))
    weights = jnp.where(allowed[:, None, :], jnp.exp(scores - newest[:, :, None]), 0.0)
    factor = jnp.exp(highest - newest)
    total = total * factor + jnp.sum(weights, axis=2)
    mixed = mixed * factor[:, :, None] + jnp.einsum(
        "qhk,khd->qhd", weights.astype(jnp.bfloat16), values, preferred_element_type=jnp.float32
    )
    return (newest, total, mixed)


def fold_keys(carry, query, piece, allowed_of):
    key_rows, values = piece
    count = key_rows.shape[0]
    head_count = query.shape[1]
    depth = query.shape[2]
    step = split_size(count, 1024)

    def inner(state, offset):
        part_keys = lax.dynamic_slice_in_dim(key_rows, offset, step, 0).reshape(
            step, head_count, depth
        )
        part_values = lax.dynamic_slice_in_dim(values, offset, step, 0).reshape(
            step, head_count, depth
        )
        index = offset + jnp.arange(step, dtype=jnp.int32)
        return (attend_block(state, query, part_keys, part_values, allowed_of(index)), None)

    offsets = jnp.arange(0, count, step, dtype=jnp.int32)
    carry, unused = lax.scan(inner, carry, offsets)
    return carry


def empty_state(row_count, head_count):
    return (
        jnp.full((row_count, head_count), NEG, jnp.float32),
        jnp.zeros((row_count, head_count), jnp.float32),
        jnp.zeros((row_count, head_count, HD), jnp.float32),
    )


def owner_combine(received, members, aslots, head_count):
    senders_top = received[0].reshape(members, aslots, head_count)
    highest = jnp.max(senders_top, axis=0)
    factor = jnp.exp(senders_top - highest[None])
    own_total = jnp.sum(received[1].reshape(members, aslots, head_count) * factor, axis=0)
    own_mixed = jnp.sum(
        received[2].reshape(members, aslots, head_count, HD) * factor[:, :, :, None], axis=0
    )
    return (own_total, own_mixed)


def shards(
    video_q,
    video_cross_keys,
    video_v,
    audio_q,
    audio_k,
    audio_v,
    audio_self_q,
    audio_self_keys,
    audio_self_v,
    video_counts,
    audio_counts,
    window_start,
    window_end,
):
    seat = lax.axis_index("seq")
    members = lax.axis_size("seq")
    width = video_q.shape[1]
    head_count = width // HD
    vslots = video_q.shape[0]
    aslots = audio_q.shape[0]
    frames_all = window_start.shape[0]
    video_index = seat * vslots + jnp.arange(vslots, dtype=jnp.int32)
    video_live, video_place = slot_info(video_counts, video_index, vslots)
    video_frame = jnp.minimum(video_place // FRAME_TOKENS, frames_all - 1)
    first_block = lookup(window_start, video_frame)
    final_block = lookup(window_end, video_frame)
    video_query = video_q.reshape(vslots, head_count, HD)

    def video_allowed(index):
        live, place = slot_info(audio_counts, index, aslots)
        block = place // AUDIO_WIN_BLOCK
        return (
            video_live[:, None]
            & live[None, :]
            & (first_block[:, None] <= block[None, :])
            & (block[None, :] < final_block[:, None])
        )

    video_state = fold_keys(
        empty_state(vslots, head_count),
        video_query,
        (
            lax.all_gather(audio_k, "seq", axis=0, tiled=True),
            lax.all_gather(audio_v, "seq", axis=0, tiled=True),
        ),
        video_allowed,
    )
    video_total = jnp.where(video_state[1] > 0, video_state[1], 1.0)
    video_result = jnp.where(
        video_live[:, None, None], video_state[2] / video_total[:, :, None], 0.0
    )
    video_out = video_result.astype(jnp.bfloat16).reshape(vslots, width)
    every_query = lax.all_gather(audio_q, "seq", axis=0, tiled=True)
    query_rows = members * aslots
    video_keys = video_cross_keys.reshape(vslots, head_count, HD)
    video_values = video_v.reshape(vslots, head_count, HD)
    query_live, query_place = slot_info(
        audio_counts, jnp.arange(query_rows, dtype=jnp.int32), aslots
    )
    query_block = query_place // AUDIO_WIN_BLOCK
    step = split_size(query_rows, 512)

    def query_part(offset):
        row_count = lax.dynamic_slice_in_dim(every_query, offset, step, 0).reshape(
            step, head_count, HD
        )
        live = lax.dynamic_slice_in_dim(query_live, offset, step, 0)
        block = lax.dynamic_slice_in_dim(query_block, offset, step, 0)
        allowed = (
            live[:, None]
            & video_live[None, :]
            & (first_block[None, :] <= block[:, None])
            & (block[:, None] < final_block[None, :])
        )
        return attend_block(
            empty_state(step, head_count), row_count, video_keys, video_values, allowed
        )

    tops, totals, mixeds = lax.map(query_part, jnp.arange(0, query_rows, step, dtype=jnp.int32))
    tops = tops.reshape(query_rows, head_count)
    totals = totals.reshape(query_rows, head_count)
    mixeds = mixeds.reshape(query_rows, width)
    received = (
        lax.all_to_all(tops, "seq", split_axis=0, concat_axis=0, tiled=True),
        lax.all_to_all(totals, "seq", split_axis=0, concat_axis=0, tiled=True),
        lax.all_to_all(mixeds, "seq", split_axis=0, concat_axis=0, tiled=True),
    )
    own_total, own_mixed = owner_combine(received, members, aslots, head_count)
    audio_index = seat * aslots + jnp.arange(aslots, dtype=jnp.int32)
    audio_live, unused_place = slot_info(audio_counts, audio_index, aslots)
    safe_total = jnp.where(own_total > 0, own_total, 1.0)
    cross = jnp.where(audio_live[:, None, None], own_mixed / safe_total[:, :, None], 0.0)
    united = (audio_self_q.reshape(aslots, head_count, HD).astype(jnp.float32) + cross).astype(
        jnp.bfloat16
    )

    def self_allowed(index):
        live, unused_position = slot_info(audio_counts, index, aslots)
        return jnp.broadcast_to(live[None, :], (aslots, index.shape[0]))

    self_state = fold_keys(
        empty_state(aslots, head_count),
        united,
        (
            lax.all_gather(audio_self_keys, "seq", axis=0, tiled=True),
            lax.all_gather(audio_self_v, "seq", axis=0, tiled=True),
        ),
        self_allowed,
    )
    attended = self_state[2] / self_state[1][:, :, None]
    audio_result = jnp.where(audio_live[:, None, None], cross + attended, 0.0)
    audio_out = audio_result.astype(jnp.bfloat16).reshape(aslots, width)
    return (video_out, audio_out)


def solution(mesh):
    return jax.shard_map(
        shards,
        mesh=mesh,
        in_specs=(
            P(("groups", "seq"), ("heads", "sub")),
            P(("groups", "seq"), ("heads", "sub")),
            P(("groups", "seq"), ("heads", "sub")),
            P(("groups", "seq"), ("heads", "sub")),
            P(("groups", "seq"), ("heads", "sub")),
            P(("groups", "seq"), ("heads", "sub")),
            P(("groups", "seq"), ("heads", "sub")),
            P(("groups", "seq"), ("heads", "sub")),
            P(("groups", "seq"), ("heads", "sub")),
            P("groups"),
            P("groups"),
            P("groups"),
            P("groups"),
        ),
        out_specs=(P(("groups", "seq"), ("heads", "sub")), P(("groups", "seq"), ("heads", "sub"))),
        check_vma=False,
    )
```

profile of v0, /device:TPU:1, one launch (start us, length us, event | category | flops | bytes accessed | tf_op | source)
XLA Modules:
  0.0 192.5 jit_solution(6322024742541215216)
XLA Ops:
  7.2 0.7 all-gather.10.cloned.1.call-update
  8.0 0.7 all-gather.6.cloned.1.call-update
  8.7 0.7 all-gather.8.cloned.1.call-update
  9.4 0.5 all-gather.12.cloned.1.call-update
  10.1 0.8 reduce-window.18
  10.9 0.7 bitcast_subtract_fusion.3
  11.6 0.7 select_reduce_fusion.5
  12.3 0.8 reduce-window.19
  13.2 0.7 bitcast_subtract_fusion.2
  13.8 0.7 select_reduce_fusion.1
  14.6 1.4 copy.87
  16.1 1.4 copy.88
  17.6 17.9 %all-gather.10.cloned.1.call-done = bf16[640,1024]{1,0:T(8,128)(2,1)} async-done(((bf16[80,1024]{1,0:T(8,128)(2,1)}), bf16[640,1024]{1,0:T(8,128)(2,1)}) %all-gather.10.cloned.1.call-update) | async-done | bytes 1310736 | tf_op jit(solution)/shard_map/all_gather | solution.py:145
  35.5 24.0 %while.2 = (s32[]{:T(128)}, f32[2,320,16]{1,0,2:T(2,128)S(1)}, f32[2,320,16]{1,0,2:T(2,128)S(1)}, f32[2,320,16,64]{1,3,2,0:T(8,128)}, s32[2]{0:T(128)S(1)}, /*in...) while((s32[]{:T(128)}, f32[2,320,16]{1,0,2:T(2,128)S(1)}, ...), condition=%wide.region_14.15_spmd, body=%wide.region_11.14_spmd.sunk | while | flops 441594880 | bytes 28242136 | solution.py:171
  35.5 0.6 dynamic_slice.32
  38.2 0.2 compare_and_fusion.3
  38.4 1.3 constant_dynamic-slice_fusion.2
  39.7 0.4 copy.118
  40.1 1.5 bitcast_reduce_fusion.3
  41.6 3.6 %bitcast_dynamic-update-slice_fusion.2 = f32[2,320,16,64]{1,3,2,0:T(8,128)} fusion(f32[2,320,16,64]{1,3,2,0:T(8,128)} %get-tuple-element.335, s32[]{:T(128)} %get-tuple-element.332, bf16[320,16,64]{0,2,1:T(8,128)(2,1)S(1)} %get-tuple-element.360, f32[16,320,320]{1,2,0:T(8,128)S(1)} %get-tuple-element.313, f32[320,16]{0,1:T(8,128)S(1)} %get-tuple-element.314, ...), kind=kOutput, calls=%fused_computation.10.clone.1 | convolution fusion | flops 218234880 | bytes 10519040 | tf_op jit(solution)/shard_map/while/body/eval_jaxpr/qhk,khd->qhd/dot_general | solution.py:45
  45.3 2.0 %fusion.92 = f32[320,16]{0,1:T(8,128)S(1)} fusion(f32[16,320,320]{1,2,0:T(8,128)S(1)} %get-tuple-element.313, f32[320,16]{0,1:T(8,128)S(1)} %get-tuple-element.314, pred[320,320]{0,1:T(8,128)(4,1)S(1)} %compare_and_fusion.3), kind=kLoop, calls=%fused_computation.6.clone.1 | loop fusion | flops 8186880 | bytes 6696960 | tf_op jit(solution)/shard_map/while/body/eval_jaxpr/reduce_sum | solution.py:44
  47.3 0.1 dynamic_update_slice.17
  47.4 0.1 dynamic_update_slice.16
  47.6 0.6 dynamic_slice.32
  50.3 0.2 compare_and_fusion.3
  50.5 1.3 constant_dynamic-slice_fusion.2
  51.8 0.4 copy.118
  52.1 1.5 bitcast_reduce_fusion.3
  53.7 3.5 %bitcast_dynamic-update-slice_fusion.2 = f32[2,320,16,64]{1,3,2,0:T(8,128)} fusion(f32[2,320,16,64]{1,3,2,0:T(8,128)} %get-tuple-element.335, s32[]{:T(128)} %get-tuple-element.332, bf16[320,16,64]{0,2,1:T(8,128)(2,1)S(1)} %get-tuple-element.360, f32[16,320,320]{1,2,0:T(8,128)S(1)} %get-tuple-element.313, f32[320,16]{0,1:T(8,128)S(1)} %get-tuple-element.314, ...), kind=kOutput, calls=%fused_computation.10.clone.1 | convolution fusion | flops 218234880 | bytes 10519040 | tf_op jit(solution)/shard_map/while/body/eval_jaxpr/qhk,khd->qhd/dot_general | solution.py:45
  57.2 2.0 %fusion.92 = f32[320,16]{0,1:T(8,128)S(1)} fusion(f32[16,320,320]{1,2,0:T(8,128)S(1)} %get-tuple-element.313, f32[320,16]{0,1:T(8,128)S(1)} %get-tuple-element.314, pred[320,320]{0,1:T(8,128)(4,1)S(1)} %compare_and_fusion.3), kind=kLoop, calls=%fused_computation.6.clone.1 | loop fusion | flops 8186880 | bytes 6696960 | tf_op jit(solution)/shard_map/while/body/eval_jaxpr/reduce_sum | solution.py:44
  59.4 0.1 dynamic_update_slice.16
  59.7 0.6 copy.93
  60.3 3.5 %all-to-all-start.1 = ((f32[8,80,16]{1,2,0:T(8,128)}), f32[8,80,16]{1,2,0:T(8,128)S(1)}, u32[]{:S(2)}, u32[]{:S(2)}) async-start(f32[8,80,16]{1,2,0:T(8,128)} %copy.93), calls=%async_computation.1 | async-start | bytes 131072 | tf_op jit(solution)/shard_map/all_to_all | solution.py:176
  64.0 0.6 copy.97
  64.6 4.3 %all-to-all-done.1 = f32[8,80,16]{1,2,0:T(8,128)S(1)} async-done(((f32[8,80,16]{1,2,0:T(8,128)}), f32[8,80,16]{1,2,0:T(8,128)S(1)}, u32[]{:S(2)}, u32[]{:S(2)}) %all-to-all-start.1) | async-done | bytes 40992 | tf_op jit(solution)/shard_map/all_to_all | solution.py:176
  69.0 4.1 %all-to-all-start.2 = ((f32[8,80,16]{1,2,0:T(8,128)}), f32[8,80,16]{1,2,0:T(8,128)S(1)}, u32[]{:S(2)}, u32[]{:S(2)}) async-start(f32[8,80,16]{1,2,0:T(8,128)} %copy.97), calls=%async_computation.2 | async-start | bytes 131072 | tf_op jit(solution)/shard_map/all_to_all | solution.py:177
  73.1 0.6 all-gather.14.cloned.1.call-update
  73.7 1.0 copy.98
  74.6 1.4 copy.85
  76.1 5.8 %copy.104 = f32[2,320,16,64]{3,2,1,0:T(8,128)} copy(f32[2,320,16,64]{1,3,2,0:T(8,128)} %get-tuple-element.128) | data formatting | bytes 5242880 | tf_op jit(solution)/shard_map/all_to_all | solution.py:178
  81.8 5.2 %reshape.498 = f32[8,80,1024]{2,1,0:T(8,128)} reshape(f32[2,320,16,64]{3,2,1,0:T(8,128)} %copy.104) | data formatting | bytes 5242880 | tf_op jit(solution)/shard_map/all_to_all | solution.py:178
  87.0 5.1 %all-to-all-start = ((f32[8,80,1024]{2,1,0:T(8,128)}), f32[8,80,1024]{2,1,0:T(8,128)S(1)}, u32[]{:S(2)}, u32[]{:S(2)}) async-start(f32[8,80,1024]{2,1,0:T(8,128)} %reshape.498), calls=%async_computation | async-start | bytes 5242880 | tf_op jit(solution)/shard_map/all_to_all | solution.py:178
  92.2 0.7 select_reduce_fusion.6
  92.9 0.5 subtract_compare_fusion
  93.5 1.7 compare_and_fusion.1
  95.1 2.4 %copy.84 = bf16[640,1024]{0,1:T(8,128)(2,1)} copy(bf16[640,1024]{1,0:T(8,128)(2,1)} %all-gather.6.cloned.1.call-done) | data formatting | bytes 2621440 | tf_op jit(solution)/shard_map/all_gather | solution.py:135
  97.5 2.4 %copy.86 = bf16[640,1024]{0,1:T(8,128)(2,1)} copy(bf16[640,1024]{1,0:T(8,128)(2,1)} %all-gather.8.cloned.1.call-done) | data formatting | bytes 2621440 | tf_op jit(solution)/shard_map/all_gather | solution.py:136
  100.0 4.2 %fusion.14 = (f32[320,16]{0,1:T(8,128)S(1)}, f32[16,640,320]{1,2,0:T(8,128)S(1)}) fusion(pred[320,640]{1,0:T(8,128)(4,1)} %compare_and_fusion.1, bf16[640,16,64]{0,2,1:T(8,128)(2,1)} %bitcast.144, bf16[320,16,64]{0,2,1:T(8,128)(2,1)S(1)} %bitcast.145), kind=kOutput, calls=%fused_computation.23 | convolution fusion | flops 429255680 | bytes 15298560 | tf_op jit(solution)/shard_map/while/body/eval_jaxpr/qhd,khd->qhk/dot_general | solution.py:37
  104.2 4.8 %fusion.15 = f32[320,16]{0,1:T(8,128)S(1)} fusion(f32[16,640,320]{1,2,0:T(8,128)S(1)} %get-tuple-element.224, f32[320,16]{0,1:T(8,128)S(1)} %broadcast_maximum_fusion.1, pred[320,640]{1,0:T(8,128)(4,1)S(1)} %copy-done.2), kind=kLoop, calls=%fused_computation.24 | loop fusion | flops 16378880 | bytes 13352960 | tf_op jit(solution)/shard_map/while/body/eval_jaxpr/reduce_sum | solution.py:44
  109.1 6.7 %fusion.34 = bf16[320,16,64]{0,2,1:T(8,128)(2,1)S(1)} fusion(bf16[640,16,64]{0,2,1:T(8,128)(2,1)S(1)} %bitcast.150, f32[16,640,320]{1,2,0:T(8,128)} %copy-done, f32[320,16]{0,1:T(8,128)S(1)} %broadcast_maximum_fusion.1, pred[320,640]{1,0:T(8,128)(4,1)S(1)} %copy-done.2, f32[320,16]{0,1:T(8,128)S(1)} %get-tuple-element.220, ...), kind=kOutput, calls=%fused_computation.46 | convolution fusion | flops 437125120 | bytes 15339840 | tf_op jit(solution)/shard_map/while/body/eval_jaxpr/qhk,khd->qhd/dot_general | solution.py:45
  115.8 1.1 copy.101
  116.9 3.0 %all-gather.12.cloned.1.call-done = bf16[640,1024]{1,0:T(8,128)(2,1)} async-done(((bf16[80,1024]{1,0:T(8,128)(2,1)}), bf16[640,1024]{1,0:T(8,128)(2,1)}) %all-gather.12.cloned.1.call-update) | async-done | bytes 1310736 | tf_op jit(solution)/shard_map/all_gather | solution.py:197
  120.0 2.5 %copy.99 = bf16[640,1024]{0,1:T(8,128)(2,1)} copy(bf16[640,1024]{1,0:T(8,128)(2,1)} %all-gather.12.cloned.1.call-done) | data formatting | bytes 2621440 | tf_op jit(solution)/shard_map/all_gather | solution.py:197
  122.5 44.5 %all-gather.14.cloned.1.call-done = bf16[640,1024]{1,0:T(8,128)(2,1)} async-done(((bf16[80,1024]{1,0:T(8,128)(2,1)}), bf16[640,1024]{1,0:T(8,128)(2,1)}) %all-gather.14.cloned.1.call-update) | async-done | bytes 1310736 | tf_op jit(solution)/shard_map/all_gather | solution.py:198
  166.9 2.4 %copy.100 = bf16[640,1024]{0,1:T(8,128)(2,1)} copy(bf16[640,1024]{1,0:T(8,128)(2,1)} %all-gather.14.cloned.1.call-done) | data formatting | bytes 2621440 | tf_op jit(solution)/shard_map/all_gather | solution.py:198
  169.4 0.1 copy.94
  169.6 3.6 %mul.131 = f32[8,80,16,64]{3,2,1,0:T(8,128)} broadcast(f32[8,80,16]{2,1,0:T(8,128)S(1)} %copy.94), dimensions={0,1,2} | broadcast | bytes 2662400 | tf_op jit(solution)/shard_map/mul | solution.py:87
  173.1 5.2 %mul.132 = f32[8,80,1024]{2,1,0:T(8,128)} reshape(f32[8,80,16,64]{3,2,1,0:T(8,128)} %mul.131) | data formatting | bytes 5242880 | tf_op jit(solution)/shard_map/mul | solution.py:87
  178.3 2.3 %multiply_reduce_fusion = f32[80,1024]{1,0:T(8,128)S(1)} fusion(f32[8,80,1024]{2,1,0:T(8,128)S(1)} %all-to-all-done, f32[8,80,1024]{2,1,0:T(8,128)} %mul.132), kind=kLoop, calls=%fused_computation.33 | loop fusion | flops 1228800 | bytes 5570560 | tf_op jit(solution)/shard_map/reduce_sum | solution.py:86
  180.6 0.2 copy.95
  180.9 2.2 %bitcast_reduce_fusion.1 = (f32[80,16]{0,1:T(8,128)S(1)}, f32[16,80,640]{2,1,0:T(8,128)S(1)}) fusion(pred[640]{0:T(1024)(128)(4,1)S(1)} %get-tuple-element.392, bf16[640,16,64]{0,2,1:T(8,128)(2,1)} %bitcast.143, f32[80,16,64]{0,2,1:T(8,128)S(1)} %bitcast.146, f32[80,16,64]{0,2,1:T(8,128)S(1)} %bitcast.147, f32[80,16]{0,1:T(8,128)S(1)} %compare_select_fusion.1, ...), kind=kOutput, calls=%fused_computation.29 | convolution fusion | flops 107641600 | bytes 5253840 | tf_op jit(solution)/shard_map/while/body/eval_jaxpr/qhd,khd->qhk/dot_general | solution.py:37
  183.0 1.0 fusion.22
  184.0 1.1 fusion.52
  185.1 0.8 copy.102
  (65 shorter events, 1.3 us)
Async XLA Ops:
  7.2 10.3 %copy-start.9 = (s32[8]{0:T(128)S(1)}, s32[8]{0:T(128)}, u32[]{:S(2)}) copy-start(s32[8]{0:T(128)} %param.26) | copy-start | bytes 100
  7.2 10.3 %copy-start.10 = (s32[8]{0:T(128)S(1)}, s32[8]{0:T(128)}, u32[]{:S(2)}) copy-start(s32[8]{0:T(128)} %param.27) | copy-start | bytes 100
  7.2 28.3 %all-gather.10.cloned.1.call-start = ((), (), s32[]{:S(2)}) async-start(), calls=%async_computation.5 | async-start | bytes 1474560 | tf_op jit(solution)/shard_map/all_gather | solution.py:145
  7.9 87.2 %all-gather.6.cloned.1.call-start = ((), (), s32[]{:S(2)}) async-start(), calls=%async_computation.3 | async-start | bytes 1474560 | tf_op jit(solution)/shard_map/all_gather | solution.py:135
  8.7 88.9 %all-gather.8.cloned.1.call-start = ((), (), s32[]{:S(2)}) async-start(), calls=%async_computation.4 | async-start | bytes 1474560 | tf_op jit(solution)/shard_map/all_gather | solution.py:136
  9.4 110.6 %all-gather.12.cloned.1.call-start = ((), (), s32[]{:S(2)}) async-start(), calls=%async_computation.6 | async-start | bytes 1474560 | tf_op jit(solution)/shard_map/all_gather | solution.py:197
  35.5 38.1 %copy-start.5 = (bf16[80,1024]{1,0:T(8,128)(2,1)S(1)}, bf16[80,1024]{1,0:T(8,128)(2,1)}, u32[]{:S(2)}) copy-start(bf16[80,1024]{1,0:T(8,128)(2,1)} %param.21) | copy-start | bytes 491524
  59.6 14.1 %copy-start.6 = (pred[320]{0:T(512)(128)(4,1)}, pred[320]{0:T(512)(128)(4,1)S(1)}, u32[]{:S(2)}) copy-start(pred[320]{0:T(512)(128)(4,1)S(1)} %get-tuple-element.393) | copy-start | bytes 964
  60.3 8.6 %all-to-all-start.1 = ((f32[8,80,16]{1,2,0:T(8,128)}), f32[8,80,16]{1,2,0:T(8,128)S(1)}, u32[]{:S(2)}, u32[]{:S(2)}) async-start(f32[8,80,16]{1,2,0:T(8,128)} %copy.93), calls=%async_computation.1 | async-start | bytes 131072 | tf_op jit(solution)/shard_map/all_to_all | solution.py:176
  69.0 18.1 %all-to-all-start.2 = ((f32[8,80,16]{1,2,0:T(8,128)}), f32[8,80,16]{1,2,0:T(8,128)S(1)}, u32[]{:S(2)}, u32[]{:S(2)}) async-start(f32[8,80,16]{1,2,0:T(8,128)} %copy.97), calls=%async_computation.2 | async-start | bytes 131072 | tf_op jit(solution)/shard_map/all_to_all | solution.py:177
  73.1 93.8 %all-gather.14.cloned.1.call-start = ((), (), s32[]{:S(2)}) async-start(), calls=%async_computation.7 | async-start | bytes 1474560 | tf_op jit(solution)/shard_map/all_gather | solution.py:198
  87.0 91.2 %all-to-all-start = ((f32[8,80,1024]{2,1,0:T(8,128)}), f32[8,80,1024]{2,1,0:T(8,128)S(1)}, u32[]{:S(2)}, u32[]{:S(2)}) async-start(f32[8,80,1024]{2,1,0:T(8,128)} %reshape.498), calls=%async_computation | async-start | bytes 5242880 | tf_op jit(solution)/shard_map/all_to_all | solution.py:178
  100.0 4.2 %copy-start.2 = (pred[320,640]{1,0:T(8,128)(4,1)S(1)}, pred[320,640]{1,0:T(8,128)(4,1)}, u32[]{:S(2)}) copy-start(pred[320,640]{1,0:T(8,128)(4,1)} %compare_and_fusion.1) | copy-start | bytes 614404
  104.2 4.9 %copy-start = (f32[16,640,320]{1,2,0:T(8,128)}, f32[16,640,320]{1,2,0:T(8,128)S(1)}, u32[]{:S(2)}) copy-start(f32[16,640,320]{1,2,0:T(8,128)S(1)} %get-tuple-element.224) | copy-start | bytes 39321604
  104.2 4.9 %copy-start.4 = (bf16[640,1024]{0,1:T(8,128)(2,1)S(1)}, bf16[640,1024]{0,1:T(8,128)(2,1)}, u32[]{:S(2)}) copy-start(bf16[640,1024]{0,1:T(8,128)(2,1)} %copy.86) | copy-start | bytes 3932164
  104.2 4.9 %copy-start.7 = (pred[320]{0:T(512)(128)(4,1)S(1)}, pred[320]{0:T(512)(128)(4,1)}, u32[]{:S(2)}) copy-start(pred[320]{0:T(512)(128)(4,1)} %copy-done.6) | copy-start | bytes 964
  178.3 2.6 %copy-start.1 = (f32[80,1024]{0,1:T(8,128)S(1)}, f32[80,1024]{0,1:T(8,128)}, u32[]{:S(2)}) copy-start(f32[80,1024]{0,1:T(8,128)} %copy.98) | copy-start | bytes 983044
  178.3 2.6 %copy-start.8 = (pred[80]{0:T(512)(128)(4,1)S(1)}, pred[80]{0:T(512)(128)(4,1)}, u32[]{:S(2)}) copy-start(pred[80]{0:T(512)(128)(4,1)} %subtract_compare_fusion) | copy-start | bytes 244
  180.8 3.2 %copy-start.3 = (bf16[640,1024]{0,1:T(8,128)(2,1)S(1)}, bf16[640,1024]{0,1:T(8,128)(2,1)}, u32[]{:S(2)}) copy-start(bf16[640,1024]{0,1:T(8,128)(2,1)} %copy.100) | copy-start | bytes 3932164
Sparse Core Ops, SparseCore 0:
  9.6 25.8 all-gather.9
  37.2 22.9 all-gather.5
  61.8 24.2 all-gather.7
  87.5 32.3 all-gather.11
  121.5 45.4 all-gather.13
where the time goes:
time: 194 us; the launch traced here: 192 us
  waiting for transfers between devices  72.9 us (38%)
  local copies, waits for them, and re-layouts  43.9 us (23%)
  matrix products  24.4 us (13%)
  other arithmetic  20.2 us (10%)
  between operations  14.1 us (7%)
  starting transfers between devices  12.9 us (7%)
  loops' own time  4.05 us (2%)
    all_gather x1, waiting for transfers between devices, shards(): lax.all_gather(audio_self_v, 'seq', axis=0, tiled=True)  44.5 us
    all_gather x1, waiting for transfers between devices, shards(): every_query = lax.all_gather(audio_q, 'seq', axis=0, tiled=True)  17.9 us
    dot_general x4, matrix products, attend_block(): jnp.einsum('qhk,khd->qhd', weights.astype(jnp.bfloat16), values, preferre...  15 us
    all_to_all x2, local copies, waits for them, and re-layouts, shards(): lax.all_to_all(mixeds, 'seq', split_axis=0, concat_axis=0, tiled=True)  10.9 us
    reduce_sum x4, other arithmetic, attend_block(): total = total * factor + jnp.sum(weights, axis=2)  9.67 us
    dot_general x4, matrix products, attend_block(): jnp.einsum('qhd,khd->qhk', query, key_rows, preferred_element_type=jnp.fl...  9.45 us
    mul x2, local copies, waits for them, and re-layouts, owner_combine(): received[2].reshape(members, aslots, head_count, HD) * factor[:, :, :, None]  8.71 us
    unnamed x27, local copies, waits for them, and re-layouts  6.32 us
  transfers between devices with their start and end apart: 8, of which 4 were waited for; matrix products, arithmetic and copies ran while one was open for 42% of the time, Pallas kernels for 0%

commit v1 on v0

v1 whole, which is shorter than its diff:
```python
import functools
import math

import jax
import jax.numpy as jnp
from jax import lax
from jax.experimental import pallas as pl
from jax.experimental.pallas import tpu as pltpu
from jax.sharding import PartitionSpec as P

HD = 64
PAIR = 128
FRAME_TOKENS = 256
AUDIO_WIN_BLOCK = 128
NEG = -1e30
FAR = 1 << 20
SCALE = HD ** (-0.5) * math.log2(math.e)
MESH = pl.DeviceIdType.MESH
Q, K, V, SK, SV = range(5)


def kernel(
    n,
    frames,
    vcount,
    acount,
    wstart,
    wend,
    vq,
    vk,
    vv,
    aq,
    ak,
    av,
    sq,
    sk,
    sv,
    vout,
    aout,
    vqs,
    vks,
    vvs,
    sqs,
    gq,
    gk,
    gv,
    gsk,
    gsv,
    vbias,
    pacc,
    pst,
    sacc,
    racc,
    rst,
    local_sem,
    send_sem,
    recv_sem,
    psend,
    precv,
):
    me = lax.axis_index("seq")
    vslots, width = vqs.shape
    aslots = sqs.shape[0]
    pairs = width // PAIR
    total = n * aslots
    bufs = (gq, gk, gv, gsk, gsv)
    owns = (aq, ak, av, sk, sv)

    fetches = []
    for t in (Q, K, V, SK, SV):
        fetches.append(pltpu.make_async_copy(owns[t], bufs[t].at[me], local_sem.at[t]))
    for i, (a, b) in enumerate(((vk, vks), (vv, vvs), (vq, vqs), (sq, sqs))):
        fetches.append(pltpu.make_async_copy(a, b, local_sem.at[5 + i]))
    for f in fetches:
        f.start()

    has_left = me > 0
    has_right = me < n - 1
    barrier = pltpu.get_barrier_semaphore()

    @pl.when(has_left)
    def _():
        pl.semaphore_signal(barrier, inc=1, device_id={"seq": me - 1}, device_id_type=MESH)

    @pl.when(has_right)
    def _():
        pl.semaphore_signal(barrier, inc=1, device_id={"seq": me + 1}, device_id_type=MESH)

    @pl.when(jnp.logical_and(has_left, has_right))
    def _():
        pl.semaphore_wait(barrier, 2)

    @pl.when(jnp.logical_not(jnp.logical_and(has_left, has_right)))
    def _():
        pl.semaphore_wait(barrier, 1)

    def relay(t, d, r):
        source = me - r if d == 0 else me + r
        target = me + 1 if d == 0 else me - 1
        return pltpu.make_async_remote_copy(
            src_ref=bufs[t].at[source],
            dst_ref=bufs[t].at[source],
            send_sem=send_sem.at[t, d, r],
            recv_sem=recv_sem.at[t, d, r + 1],
            device_id={"seq": target},
            device_id_type=MESH,
        )

    def have(d, r):
        return me - r >= 0 if d == 0 else me + r <= n - 1

    def passes(d):
        return has_right if d == 0 else has_left

    def arrived(t, d, r):
        source = me - r if d == 0 else me + r
        pltpu.make_async_copy(
            bufs[t].at[source], bufs[t].at[source], recv_sem.at[t, d, r]
        ).wait()

    def forward(t, r, first=False):
        for d in (0, 1):

            @pl.when(have(d, r))
            def _():
                if not first:
                    arrived(t, d, r)

                @pl.when(passes(d))
                def _():
                    relay(t, d, r).start()

    def sent(t, r):
        for d in (0, 1):

            @pl.when(jnp.logical_and(have(d, r), passes(d)))
            def _():
                relay(t, d, r).wait_send()

    for t in (Q, K, V):
        fetches[t].wait()
        forward(t, 0, True)

    lane = lax.broadcasted_iota(jnp.int32, (1, PAIR), 1)
    low = lane < HD
    keep = (
        jnp.where(low, 1.0, 0.0).astype(jnp.bfloat16),
        jnp.where(low, 0.0, 1.0).astype(jnp.bfloat16),
    )

    def start_of(counts, index):
        at = jnp.int32(0)
        for s in range(n):
            at = at + jnp.where(s < index, counts[s], 0)
        return at

    def video_window(place):
        position = start_of(vcount, me) + place
        live = place < vcount[me]
        frame = position // FRAME_TOKENS
        first = jnp.full(place.shape, FAR, jnp.int32)
        final = jnp.zeros(place.shape, jnp.int32)
        for f in range(frames):
            here = jnp.logical_and(frame == f, live)
            first = jnp.where(here, wstart[f], first)
            final = jnp.where(here, wend[f], final)
        return first, final

    def weigh(query, key_rows, values, bias):
        score = (
            lax.dot_general(
                query, key_rows, (((1,), (1,)), ((), ())), preferred_element_type=jnp.float32
            )
            * SCALE
            + bias
        )
        top = jnp.max(score, axis=1, keepdims=True)
        weight = jnp.exp2(score - top)
        mass = jnp.sum(weight, axis=1, keepdims=True)
        mixed = jnp.dot(
            weight.astype(jnp.bfloat16), values, preferred_element_type=jnp.float32
        )
        return top, mass, mixed

    first_row, final_row = video_window(lax.broadcasted_iota(jnp.int32, (1, vslots), 1))
    video_place = lax.broadcasted_iota(jnp.int32, (vslots, 1), 0)
    first_col, final_col = video_window(video_place)
    audio_index = lax.broadcasted_iota(jnp.int32, (1, total), 1)
    audio_block = jnp.full((1, total), -1, jnp.int32)
    begin = jnp.int32(0)
    for s in range(n):
        place = audio_index - s * aslots
        here = jnp.logical_and(place >= 0, place < acount[s])
        audio_block = jnp.where(here, (begin + place) // AUDIO_WIN_BLOCK, audio_block)
        begin = begin + acount[s]
    vbias[...] = jnp.where(
        jnp.logical_and(first_col <= audio_block, audio_block < final_col), 0.0, NEG
    )
    self_bias = jnp.where(audio_block >= 0, 0.0, NEG)
    audio_place = lax.broadcasted_iota(jnp.int32, (aslots, 1), 0)

    def columns(p):
        return pl.ds(pl.multiple_of(p * PAIR, PAIR), PAIR)

    def audio_cross(j):
        block = jnp.where(
            audio_place < acount[j],
            (start_of(acount, j) + audio_place) // AUDIO_WIN_BLOCK,
            -1,
        )
        bias = jnp.where(
            jnp.logical_and(first_row <= block, block < final_row), 0.0, NEG
        )

        def step(p, stats):
            cols = columns(p)
            query = gq[j, :, cols]
            key_rows = vks[:, cols]
            values = vvs[:, cols]
            parts = []
            for h in (0, 1):
                top, mass, mixed = weigh(query * keep[h], key_rows, values, bias)
                stats = jnp.where(lane == 2 * p + h, top, stats)
                stats = jnp.where(lane == HD + 2 * p + h, mass, stats)
                parts.append(mixed)
            pacc[j, :, cols] = jnp.where(low, parts[0], parts[1])
            return stats

        pst[j] = lax.fori_loop(
            0, pairs, step, jnp.zeros((aslots, PAIR), jnp.float32), unroll=min(4, pairs)
        )

    fetches[5].wait()
    fetches[6].wait()

    def first_round(r, carry):
        @pl.when(r > 0)
        def _():
            for t in (Q, K, V):
                forward(t, r)

        @pl.when(have(0, r))
        def _():
            audio_cross(me - r)

        @pl.when(jnp.logical_and(have(1, r), r > 0))
        def _():
            audio_cross(me + r)

        return carry

    lax.fori_loop(0, n, first_round, 0)
    fetches[SK].wait()
    fetches[SV].wait()
    fetches[7].wait()
    fetches[8].wait()

    def merge(d, j):
        mine = pst[j]
        other = rst[d, j]
        top = jnp.maximum(mine, other)
        a = jnp.exp2(mine - top)
        b = jnp.exp2(other - top)
        mass = mine * pltpu.roll(a, HD, 1) + other * pltpu.roll(b, HD, 1)
        pst[j] = jnp.where(low, top, mass)
        for p in range(pairs):
            cols = pl.ds(p * PAIR, PAIR)
            wa = jnp.where(low, a[:, 2 * p : 2 * p + 1], a[:, 2 * p + 1 : 2 * p + 2])
            wb = jnp.where(low, b[:, 2 * p : 2 * p + 1], b[:, 2 * p + 1 : 2 * p + 2])
            pacc[j, :, cols] = pacc[j, :, cols] * wa + racc[d, j, :, cols].astype(
                jnp.float32
            ) * wb

    def pushes(d, j):
        target = me + 1 if d == 0 else me - 1
        return [
            pltpu.make_async_remote_copy(
                src_ref=src.at[j],
                dst_ref=dst.at[d, j],
                send_sem=psend.at[d, i, j],
                recv_sem=precv.at[d, i, j],
                device_id={"seq": target},
                device_id_type=MESH,
            )
            for i, (src, dst) in enumerate(((sacc, racc), (pst, rst)))
        ]

    def chain(d, step):
        lag = me if d == 0 else n - 1 - me
        j = n - 1 - step + me if d == 0 else step - (n - 1 - me)

        @pl.when(step >= lag)
        def _():
            @pl.when(passes(1 - d))
            def _():
                for i, dst in enumerate((racc, rst)):
                    pltpu.make_async_copy(
                        dst.at[d, j], dst.at[d, j], precv.at[d, i, j]
                    ).wait()
                merge(d, j)

            @pl.when(j != me)
            def _():
                sacc[j] = pacc[j].astype(jnp.bfloat16)
                for c in pushes(d, j):
                    c.start()

    video_live = video_place < vcount[me]
    chunk = 160 if vslots % 160 == 0 else vslots

    def video_pair(p, carry):
        cols = columns(p)
        key_rows = gk[:, :, cols].reshape(total, PAIR)
        values = gv[:, :, cols].reshape(total, PAIR)
        for c in range(vslots // chunk):
            rows = pl.ds(c * chunk, chunk)
            query = vqs[rows, cols]
            bias = vbias[rows, :]
            parts = []
            for h in (0, 1):
                top, mass, mixed = weigh(query * keep[h], key_rows, values, bias)
                parts.append(mixed / mass)
            result = jnp.where(low, parts[0], parts[1])
            live = video_live[c * chunk : (c + 1) * chunk]
            vout[rows, cols] = jnp.where(live, result, 0.0).astype(jnp.bfloat16)
        return carry

    per_step = -(-pairs // n)

    def second_round(r, carry):
        @pl.when(r == 0)
        def _():
            forward(SK, 0, True)
            forward(SV, 0, True)

        @pl.when(r > 0)
        def _():
            forward(SK, r)
            forward(SV, r)

        chain(0, r)
        chain(1, r)
        for i in range(per_step):

            @pl.when(r * per_step + i < pairs)
            def _():
                video_pair(r * per_step + i, 0)

        return carry

    lax.fori_loop(0, n, second_round, 0)

    audio_live = audio_place < acount[me]
    stats = pst[me]
    for p in range(pairs):
        cols = pl.ds(p * PAIR, PAIR)
        mass = jnp.where(
            low,
            stats[:, HD + 2 * p : HD + 2 * p + 1],
            stats[:, HD + 2 * p + 1 : HD + 2 * p + 2],
        )
        cross = jnp.where(audio_live, pacc[me, :, cols] / mass, 0.0)
        united = (sqs[:, cols].astype(jnp.float32) + cross).astype(jnp.bfloat16)
        key_rows = gsk[:, :, cols].reshape(total, PAIR)
        values = gsv[:, :, cols].reshape(total, PAIR)
        parts = []
        for h in (0, 1):
            top, own_mass, mixed = weigh(united * keep[h], key_rows, values, self_bias)
            parts.append(mixed / own_mass)
        attended = jnp.where(low, parts[0], parts[1])
        aout[:, cols] = jnp.where(audio_live, cross + attended, 0.0).astype(jnp.bfloat16)

    def drain(r, carry):
        for t in (Q, K, V, SK, SV):
            sent(t, r)
        for d in (0, 1):
            ahead = r > me if d == 0 else r < me

            @pl.when(ahead)
            def _():
                for c in pushes(d, r):
                    c.wait_send()

        return carry

    lax.fori_loop(0, n, drain, 0)


def solution(mesh):
    n = mesh.shape["seq"]

    def shards(*arrays):
        vslots, width = arrays[0].shape
        aslots = arrays[3].shape[0]
        frames = arrays[11].shape[0]
        smem = pl.BlockSpec(memory_space=pltpu.SMEM)
        anywhere = pl.BlockSpec(memory_space=pl.ANY)
        vmem = pl.BlockSpec(memory_space=pltpu.VMEM)
        half, full = jnp.bfloat16, jnp.float32
        return pl.pallas_call(
            functools.partial(kernel, n, frames),
            name="attend",
            out_shape=(
                jax.ShapeDtypeStruct((vslots, width), half),
                jax.ShapeDtypeStruct((aslots, width), half),
            ),
            in_specs=[smem] * 4 + [anywhere] * 9,
            out_specs=(vmem, vmem),
            scratch_shapes=[pltpu.VMEM((vslots, width), half)] * 3
            + [pltpu.VMEM((aslots, width), half)]
            + [pltpu.VMEM((n, aslots, width), half)] * 5
            + [
                pltpu.VMEM((vslots, n * aslots), full),
                pltpu.VMEM((n, aslots, width), full),
                pltpu.VMEM((n, aslots, PAIR), full),
                pltpu.VMEM((n, aslots, width), half),
                pltpu.VMEM((2, n, aslots, width), half),
                pltpu.VMEM((2, n, aslots, PAIR), full),
                pltpu.SemaphoreType.DMA((9,)),
                pltpu.SemaphoreType.DMA((5, 2, n)),
                pltpu.SemaphoreType.DMA((5, 2, n + 1)),
                pltpu.SemaphoreType.DMA((2, 2, n)),
                pltpu.SemaphoreType.DMA((2, 2, n)),
            ],
            compiler_params=pltpu.CompilerParams(
                collective_id=0, has_side_effects=True, vmem_limit_bytes=56 << 20
            ),
        )(*arrays[9:], *arrays[:9])

    rows = P(("groups", "seq"), ("heads", "sub"))
    return jax.shard_map(
        shards,
        mesh=mesh,
        in_specs=(rows,) * 9 + (P("groups"),) * 4,
        out_specs=(rows, rows),
        check_vma=False,
    )
```

time: 194 us -> 98 us (0.51)
  Pallas kernels: 0 us -> 94.1 us
  waiting for transfers between devices: 72.9 us -> 0 us
  local copies, waits for them, and re-layouts: 43.9 us -> 2.67 us
  matrix products: 24.4 us -> 0 us
  other arithmetic: 20.2 us -> 0 us
  between operations: 14.1 us -> 0.65 us
  starting transfers between devices: 12.9 us -> 0 us
  loops' own time: 4.05 us -> 0 us
    pallas_call x0 -> x1, Pallas kernels: none -> 94.1 us  [shards(): pl.pallas_call(functools.partial(kernel, n, frames), name='attend', out_s...]
    all_gather x5 -> x0, waiting for transfers between devices: 65.4 us -> none  [the longest x1 44.5 us: shards(): lax.all_gather(audio_self_v, 'seq', axis=0, tiled=True)]
    dot_general x8 -> x0, matrix products: 24.4 us -> none  [the longest x4 15 us: attend_block(): jnp.einsum('qhk,khd->qhd', weights.astype(jnp.bfloat16), values, preferre...]
    reduce_sum x10 -> x0, other arithmetic: 14.3 us -> none  [the longest x4 9.67 us: attend_block(): total = total * factor + jnp.sum(weights, axis=2)]
    all_to_all x3 -> x0, starting transfers between devices: 12.8 us -> none  [the longest x1 5.14 us: shards(): lax.all_to_all(mixeds, 'seq', split_axis=0, concat_axis=0, tiled=True)]
    all_to_all x6 -> x0, local copies, waits for them, and re-layouts: 12.5 us -> none  [the longest x2 10.9 us: shards(): lax.all_to_all(mixeds, 'seq', split_axis=0, concat_axis=0, tiled=True)]
    all_gather x4 -> x0, local copies, waits for them, and re-layouts: 9.8 us -> none  [the longest x1 2.49 us: shards(): lax.all_gather(audio_self_keys, 'seq', axis=0, tiled=True)]
    mul x2 -> x0, local copies, waits for them, and re-layouts: 8.71 us -> none  [owner_combine(): received[2].reshape(members, aslots, head_count, HD) * factor[:, :, :, None]]
  transfers between devices with their start and end apart: 8 -> 0, of which waited for: 4 -> 0; matrix products, arithmetic and copies ran while one was open for 42% -> 0% of each run, Pallas kernels for 0% -> 0%
where the time goes in v1:
time: 98 us; the launch traced here: 97.5 us
  Pallas kernels  94.1 us (96%)
  local copies, waits for them, and re-layouts  2.67 us (3%)
    pallas_call x1, Pallas kernels, shards(): pl.pallas_call(functools.partial(kernel, n, frames), name='attend', out_s...  94.1 us
    unnamed x4, local copies, waits for them, and re-layouts  2.67 us

profile of v1, /device:TPU:1, one launch (start us, length us, event | category | flops | bytes accessed | tf_op | source)
XLA Modules:
  0.0 97.5 jit_solution(9218673194744875440)
XLA Ops:
  0.6 94.1 %attend.1 = (bf16[320,1024]{1,0:T(8,128)(2,1)}, bf16[80,1024]{1,0:T(8,128)(2,1)}) custom-call(s32[8]{0:T(128)} %vcount.1, s32[8]{0:T(128)} %acount.1, s32[8]{0:T(128)} %wstart.1, s32[8]{0:T(128)} %wend.1, bf16[320,1024]{1,0:T(8,128)(2,1)} %vq.1, bf16[320,1024]{1,0:T(8,128)(2,1)} %vk.1, bf16[320,1024]{1,0:T(8,128)(2,1)} %vv.1, bf16[80,1024]{1,0:T(8,128)(2,1)} %aq.1, ...), custom_call_target="tpu_custom_call" | custom-call | tf_op jit(solution)/shard_map/attend/pallas_call | solution.py:400
  94.8 0.0 copy-start
  94.8 2.0 %copy.17 = bf16[320,1024]{1,0:T(8,128)(2,1)} copy(bf16[320,1024]{1,0:T(8,128)(2,1)} %get-tuple-element.4) | data formatting | bytes 1310720
  96.8 0.0 copy-done
  96.8 0.7 copy.18
Async XLA Ops:
  94.8 2.0 %copy-start = (bf16[80,1024]{1,0:T(8,128)(2,1)S(1)}, bf16[80,1024]{1,0:T(8,128)(2,1)}, u32[]{:S(2)}) copy-start(bf16[80,1024]{1,0:T(8,128)(2,1)} %get-tuple-element.5) | copy-start | bytes 491524

commit v2 on v1

--- a/solution.py
+++ b/solution.py
@@ -167,20 +167,21 @@
         return first, final
 
     def weigh(query, key_rows, values, bias):
-        score = (
-            lax.dot_general(
-                query, key_rows, (((1,), (1,)), ((), ())), preferred_element_type=jnp.float32
-            )
-            * SCALE
-            + bias
-        )
-        top = jnp.max(score, axis=1, keepdims=True)
+        rows = query.shape[0]
+        both = jnp.concatenate([query * keep[0], query * keep[1]], axis=0)
+        score = lax.dot_general(
+            both, key_rows, (((1,), (1,)), ((), ())), preferred_element_type=jnp.float32
+        )
+        score = score.reshape(2, rows, key_rows.shape[0]) * SCALE + bias[None]
+        top = jnp.max(score, axis=2, keepdims=True)
         weight = jnp.exp2(score - top)
-        mass = jnp.sum(weight, axis=1, keepdims=True)
+        mass = jnp.sum(weight, axis=2, keepdims=True)
         mixed = jnp.dot(
-            weight.astype(jnp.bfloat16), values, preferred_element_type=jnp.float32
-        )
-        return top, mass, mixed
+            weight.astype(jnp.bfloat16).reshape(2 * rows, key_rows.shape[0]),
+            values,
+            preferred_element_type=jnp.float32,
+        )
+        return top, mass, jnp.where(low, mixed[:rows], mixed[rows:])
 
     first_row, final_row = video_window(lax.broadcasted_iota(jnp.int32, (1, vslots), 1))
     video_place = lax.broadcasted_iota(jnp.int32, (vslots, 1), 0)
@@ -217,13 +218,11 @@
             query = gq[j, :, cols]
             key_rows = vks[:, cols]
             values = vvs[:, cols]
-            parts = []
+            top, mass, mixed = weigh(query, key_rows, values, bias)
             for h in (0, 1):
-                top, mass, mixed = weigh(query * keep[h], key_rows, values, bias)
-                stats = jnp.where(lane == 2 * p + h, top, stats)
-                stats = jnp.where(lane == HD + 2 * p + h, mass, stats)
-                parts.append(mixed)
-            pacc[j, :, cols] = jnp.where(low, parts[0], parts[1])
+                stats = jnp.where(lane == 2 * p + h, top[h], stats)
+                stats = jnp.where(lane == HD + 2 * p + h, mass[h], stats)
+            pacc[j, :, cols] = mixed
             return stats
 
         pst[j] = lax.fori_loop(
@@ -316,11 +315,8 @@
             rows = pl.ds(c * chunk, chunk)
             query = vqs[rows, cols]
             bias = vbias[rows, :]
-            parts = []
-            for h in (0, 1):
-                top, mass, mixed = weigh(query * keep[h], key_rows, values, bias)
-                parts.append(mixed / mass)
-            result = jnp.where(low, parts[0], parts[1])
+            top, mass, mixed = weigh(query, key_rows, values, bias)
+            result = mixed / jnp.where(low, mass[0], mass[1])
             live = video_live[c * chunk : (c + 1) * chunk]
             vout[rows, cols] = jnp.where(live, result, 0.0).astype(jnp.bfloat16)
         return carry
@@ -363,11 +359,8 @@
         united = (sqs[:, cols].astype(jnp.float32) + cross).astype(jnp.bfloat16)
         key_rows = gsk[:, :, cols].reshape(total, PAIR)
         values = gsv[:, :, cols].reshape(total, PAIR)
-        parts = []
-        for h in (0, 1):
-            top, own_mass, mixed = weigh(united * keep[h], key_rows, values, self_bias)
-            parts.append(mixed / own_mass)
-        attended = jnp.where(low, parts[0], parts[1])
+        top, own_mass, mixed = weigh(united, key_rows, values, self_bias)
+        attended = mixed / jnp.where(low, own_mass[0], own_mass[1])
         aout[:, cols] = jnp.where(audio_live, cross + attended, 0.0).astype(jnp.bfloat16)
 
     def drain(r, carry):

time: 98 us -> 85.9 us (0.88)
  Pallas kernels: 94.1 us -> 81.8 us
    pallas_call x1, Pallas kernels: 94.1 us -> 81.8 us  [shards(): pl.pallas_call(functools.partial(kernel, n, frames), name='attend', out_s...]
where the time goes in v2:
time: 85.9 us; the launch traced here: 85.1 us
  Pallas kernels  81.8 us (95%)
  local copies, waits for them, and re-layouts  2.67 us (3%)
    pallas_call x1, Pallas kernels, shards(): pl.pallas_call(functools.partial(kernel, n, frames), name='attend', out_s...  81.8 us
    unnamed x4, local copies, waits for them, and re-layouts  2.67 us

profile of v2, /device:TPU:1, one launch (start us, length us, event | category | flops | bytes accessed | tf_op | source)
XLA Modules:
  0.0 85.1 jit_solution(11915924289654356734)
XLA Ops:
  0.6 81.8 %attend.1 = (bf16[320,1024]{1,0:T(8,128)(2,1)}, bf16[80,1024]{1,0:T(8,128)(2,1)}) custom-call(s32[8]{0:T(128)} %vcount.1, s32[8]{0:T(128)} %acount.1, s32[8]{0:T(128)} %wstart.1, s32[8]{0:T(128)} %wend.1, bf16[320,1024]{1,0:T(8,128)(2,1)} %vq.1, bf16[320,1024]{1,0:T(8,128)(2,1)} %vk.1, bf16[320,1024]{1,0:T(8,128)(2,1)} %vv.1, bf16[80,1024]{1,0:T(8,128)(2,1)} %aq.1, ...), custom_call_target="tpu_custom_call" | custom-call | tf_op jit(solution)/shard_map/attend/pallas_call | solution.py:393
  82.4 0.0 copy-start
  82.4 2.0 %copy.17 = bf16[320,1024]{1,0:T(8,128)(2,1)} copy(bf16[320,1024]{1,0:T(8,128)(2,1)} %get-tuple-element.4) | data formatting | bytes 1310720
  84.4 0.0 copy-done
  84.4 0.7 copy.18
Async XLA Ops:
  82.4 2.0 %copy-start = (bf16[80,1024]{1,0:T(8,128)(2,1)S(1)}, bf16[80,1024]{1,0:T(8,128)(2,1)}, u32[]{:S(2)}) copy-start(bf16[80,1024]{1,0:T(8,128)(2,1)} %get-tuple-element.5) | copy-start | bytes 491524

commit v3 on v2

--- a/solution.py
+++ b/solution.py
@@ -231,17 +231,34 @@
 
     fetches[5].wait()
     fetches[6].wait()
+    fetches[SK].wait()
+    fetches[SV].wait()
+    early = n // 2 + 1 if n > 2 else n - 1
 
     def first_round(r, carry):
         @pl.when(r > 0)
         def _():
-            for t in (Q, K, V):
-                forward(t, r)
+            forward(Q, r)
 
         @pl.when(have(0, r))
         def _():
             audio_cross(me - r)
 
+        @pl.when(r > 0)
+        def _():
+            forward(K, r)
+            forward(V, r)
+
+        @pl.when(r == early)
+        def _():
+            forward(SK, 0, True)
+            forward(SV, 0, True)
+
+        @pl.when(r > early)
+        def _():
+            forward(SK, r - early)
+            forward(SV, r - early)
+
         @pl.when(jnp.logical_and(have(1, r), r > 0))
         def _():
             audio_cross(me + r)
@@ -249,60 +266,75 @@
         return carry
 
     lax.fori_loop(0, n, first_round, 0)
-    fetches[SK].wait()
-    fetches[SV].wait()
     fetches[7].wait()
     fetches[8].wait()
 
-    def merge(d, j):
-        mine = pst[j]
-        other = rst[d, j]
-        top = jnp.maximum(mine, other)
-        a = jnp.exp2(mine - top)
-        b = jnp.exp2(other - top)
-        mass = mine * pltpu.roll(a, HD, 1) + other * pltpu.roll(b, HD, 1)
-        pst[j] = jnp.where(low, top, mass)
-        for p in range(pairs):
-            cols = pl.ds(p * PAIR, PAIR)
-            wa = jnp.where(low, a[:, 2 * p : 2 * p + 1], a[:, 2 * p + 1 : 2 * p + 2])
-            wb = jnp.where(low, b[:, 2 * p : 2 * p + 1], b[:, 2 * p + 1 : 2 * p + 2])
-            pacc[j, :, cols] = pacc[j, :, cols] * wa + racc[d, j, :, cols].astype(
-                jnp.float32
-            ) * wb
-
-    def pushes(d, j):
+    halves = 2 if pairs % 2 == 0 else 1
+    half_pairs = pairs // halves
+
+    def piece(h):
+        return pl.ds(h * half_pairs * PAIR, half_pairs * PAIR)
+
+    def push(d, i, j):
         target = me + 1 if d == 0 else me - 1
-        return [
-            pltpu.make_async_remote_copy(
-                src_ref=src.at[j],
-                dst_ref=dst.at[d, j],
-                send_sem=psend.at[d, i, j],
-                recv_sem=precv.at[d, i, j],
-                device_id={"seq": target},
-                device_id_type=MESH,
-            )
-            for i, (src, dst) in enumerate(((sacc, racc), (pst, rst)))
-        ]
+        if i == 0:
+            src, dst = pst.at[j], rst.at[d, j]
+        else:
+            src, dst = sacc.at[j, :, piece(i - 1)], racc.at[d, j, :, piece(i - 1)]
+        return pltpu.make_async_remote_copy(
+            src_ref=src,
+            dst_ref=dst,
+            send_sem=psend.at[d, i, j],
+            recv_sem=precv.at[d, i, j],
+            device_id={"seq": target},
+            device_id_type=MESH,
+        )
+
+    def landed(d, i, j):
+        dst = rst.at[d, j] if i == 0 else racc.at[d, j, :, piece(i - 1)]
+        pltpu.make_async_copy(dst, dst, precv.at[d, i, j]).wait()
 
     def chain(d, step):
         lag = me if d == 0 else n - 1 - me
         j = n - 1 - step + me if d == 0 else step - (n - 1 - me)
-
-        @pl.when(step >= lag)
-        def _():
-            @pl.when(passes(1 - d))
+        receives = passes(1 - d)
+        moves_on = j != me
+
+        @pl.when(jnp.logical_and(step >= lag, jnp.logical_and(moves_on, jnp.logical_not(receives))))
+        def _():
+            push(d, 0, j).start()
+            for h in range(halves):
+                sacc[j, :, piece(h)] = pacc[j, :, piece(h)].astype(jnp.bfloat16)
+                push(d, h + 1, j).start()
+
+        @pl.when(jnp.logical_and(step >= lag, receives))
+        def _():
+            landed(d, 0, j)
+            mine = pst[j]
+            other = rst[d, j]
+            top = jnp.maximum(mine, other)
+            a = jnp.exp2(mine - top)
+            b = jnp.exp2(other - top)
+            mass = mine * pltpu.roll(a, HD, 1) + other * pltpu.roll(b, HD, 1)
+            pst[j] = jnp.where(low, top, mass)
+
+            @pl.when(moves_on)
             def _():
-                for i, dst in enumerate((racc, rst)):
-                    pltpu.make_async_copy(
-                        dst.at[d, j], dst.at[d, j], precv.at[d, i, j]
-                    ).wait()
-                merge(d, j)
-
-            @pl.when(j != me)
-            def _():
-                sacc[j] = pacc[j].astype(jnp.bfloat16)
-                for c in pushes(d, j):
-                    c.start()
+                push(d, 0, j).start()
+
+            for h in range(halves):
+                landed(d, h + 1, j)
+                for p in range(h * half_pairs, (h + 1) * half_pairs):
+                    cols = pl.ds(p * PAIR, PAIR)
+                    wa = jnp.where(low, a[:, 2 * p : 2 * p + 1], a[:, 2 * p + 1 : 2 * p + 2])
+                    wb = jnp.where(low, b[:, 2 * p : 2 * p + 1], b[:, 2 * p + 1 : 2 * p + 2])
+                    merged = pacc[j, :, cols] * wa + racc[d, j, :, cols].astype(jnp.float32) * wb
+                    pacc[j, :, cols] = merged
+                    sacc[j, :, cols] = merged.astype(jnp.bfloat16)
+
+                @pl.when(moves_on)
+                def _():
+                    push(d, h + 1, j).start()
 
     video_live = video_place < vcount[me]
     chunk = 160 if vslots % 160 == 0 else vslots
@@ -324,15 +356,10 @@
     per_step = -(-pairs // n)
 
     def second_round(r, carry):
-        @pl.when(r == 0)
-        def _():
-            forward(SK, 0, True)
-            forward(SV, 0, True)
-
-        @pl.when(r > 0)
-        def _():
-            forward(SK, r)
-            forward(SV, r)
+        @pl.when(r < early)
+        def _():
+            forward(SK, r + n - early)
+            forward(SV, r + n - early)
 
         chain(0, r)
         chain(1, r)
@@ -371,8 +398,8 @@
 
             @pl.when(ahead)
             def _():
-                for c in pushes(d, r):
-                    c.wait_send()
+                for i in range(halves + 1):
+                    push(d, i, r).wait_send()
 
         return carry
 
@@ -412,8 +439,8 @@
                 pltpu.SemaphoreType.DMA((9,)),
                 pltpu.SemaphoreType.DMA((5, 2, n)),
                 pltpu.SemaphoreType.DMA((5, 2, n + 1)),
-                pltpu.SemaphoreType.DMA((2, 2, n)),
-                pltpu.SemaphoreType.DMA((2, 2, n)),
+                pltpu.SemaphoreType.DMA((2, 3, n)),
+                pltpu.SemaphoreType.DMA((2, 3, n)),
             ],
             compiler_params=pltpu.CompilerParams(
                 collective_id=0, has_side_effects=True, vmem_limit_bytes=56 << 20

time: 85.9 us -> 84.2 us (0.980)
  Pallas kernels: 81.8 us -> 80 us
    pallas_call x1, Pallas kernels: 81.8 us -> 80 us  [shards(): pl.pallas_call(functools.partial(kernel, n, frames), name='attend', out_s...]
where the time goes in v3:
time: 84.2 us; the launch traced here: 83.3 us
  Pallas kernels  80 us (95%)
  local copies, waits for them, and re-layouts  2.67 us (3%)
    pallas_call x1, Pallas kernels, shards(): pl.pallas_call(functools.partial(kernel, n, frames), name='attend', out_s...  80 us
    unnamed x4, local copies, waits for them, and re-layouts  2.67 us

profile of v3, /device:TPU:1, one launch (start us, length us, event | category | flops | bytes accessed | tf_op | source)
XLA Modules:
  0.0 83.3 jit_solution(9155017931855668912)
XLA Ops:
  0.6 80.0 %attend.1 = (bf16[320,1024]{1,0:T(8,128)(2,1)}, bf16[80,1024]{1,0:T(8,128)(2,1)}) custom-call(s32[8]{0:T(128)} %vcount.1, s32[8]{0:T(128)} %acount.1, s32[8]{0:T(128)} %wstart.1, s32[8]{0:T(128)} %wend.1, bf16[320,1024]{1,0:T(8,128)(2,1)} %vq.1, bf16[320,1024]{1,0:T(8,128)(2,1)} %vk.1, bf16[320,1024]{1,0:T(8,128)(2,1)} %vv.1, bf16[80,1024]{1,0:T(8,128)(2,1)} %aq.1, ...), custom_call_target="tpu_custom_call" | custom-call | tf_op jit(solution)/shard_map/attend/pallas_call | solution.py:420
  80.7 0.0 copy-start
  80.7 2.0 %copy.17 = bf16[320,1024]{1,0:T(8,128)(2,1)} copy(bf16[320,1024]{1,0:T(8,128)(2,1)} %get-tuple-element.4) | data formatting | bytes 1310720
  82.7 0.0 copy-done
  82.7 0.7 copy.18
Async XLA Ops:
  80.7 2.0 %copy-start = (bf16[80,1024]{1,0:T(8,128)(2,1)S(1)}, bf16[80,1024]{1,0:T(8,128)(2,1)}, u32[]{:S(2)}) copy-start(bf16[80,1024]{1,0:T(8,128)(2,1)} %get-tuple-element.5) | copy-start | bytes 491524

commit v4 on v3

--- a/solution.py
+++ b/solution.py
@@ -356,13 +356,14 @@
     per_step = -(-pairs // n)
 
     def second_round(r, carry):
+        chain(0, r)
+        chain(1, r)
+
         @pl.when(r < early)
         def _():
             forward(SK, r + n - early)
             forward(SV, r + n - early)
 
-        chain(0, r)
-        chain(1, r)
         for i in range(per_step):
 
             @pl.when(r * per_step + i < pairs)

time: 84.2 us -> 83.4 us (level)
  no operation moved by 1% of the time
where the time goes in v4:
time: 83.4 us; the launch traced here: 83.2 us
  Pallas kernels  79.9 us (96%)
  local copies, waits for them, and re-layouts  2.67 us (3%)
    pallas_call x1, Pallas kernels, shards(): pl.pallas_call(functools.partial(kernel, n, frames), name='attend', out_s...  79.9 us
    unnamed x4, local copies, waits for them, and re-layouts  2.67 us

profile of v4, /device:TPU:1, one launch (start us, length us, event | category | flops | bytes accessed | tf_op | source)
XLA Modules:
  0.0 83.2 jit_solution(11357243330780377658)
XLA Ops:
  0.6 79.9 %attend.1 = (bf16[320,1024]{1,0:T(8,128)(2,1)}, bf16[80,1024]{1,0:T(8,128)(2,1)}) custom-call(s32[8]{0:T(128)} %vcount.1, s32[8]{0:T(128)} %acount.1, s32[8]{0:T(128)} %wstart.1, s32[8]{0:T(128)} %wend.1, bf16[320,1024]{1,0:T(8,128)(2,1)} %vq.1, bf16[320,1024]{1,0:T(8,128)(2,1)} %vk.1, bf16[320,1024]{1,0:T(8,128)(2,1)} %vv.1, bf16[80,1024]{1,0:T(8,128)(2,1)} %aq.1, ...), custom_call_target="tpu_custom_call" | custom-call | tf_op jit(solution)/shard_map/attend/pallas_call | solution.py:421
  80.6 0.0 copy-start
  80.6 2.0 %copy.17 = bf16[320,1024]{1,0:T(8,128)(2,1)} copy(bf16[320,1024]{1,0:T(8,128)(2,1)} %get-tuple-element.4) | data formatting | bytes 1310720
  82.6 0.0 copy-done
  82.6 0.7 copy.18
Async XLA Ops:
  80.6 2.0 %copy-start = (bf16[80,1024]{1,0:T(8,128)(2,1)S(1)}, bf16[80,1024]{1,0:T(8,128)(2,1)}, u32[]{:S(2)}) copy-start(bf16[80,1024]{1,0:T(8,128)(2,1)} %get-tuple-element.5) | copy-start | bytes 491524
